TPU v7x, 256 devices: a whole 4x4x8 slice. The times are simulated.
256 devices in a mesh: gx: 64 (over z, y, x_hi), gy: 4 (over x_lo, core).
Axes of the slice: x: 4 (x_hi: 2, x_lo: 2; x = x_hi * 2 + x_lo), y: 4, z: 8, core: 2. Of those that a mesh axis runs over, the one named last changes fastest.
Arguments:
- points: bfloat16 [4, 64, 64, 32, 128], P('gy', 'gx'), may hold values from -6 to 6
- counts: int32 [4, 64, 64], P('gy', 'gx'), may hold values from 10 to 32, as said below
- voxels: int32 [4, 64, 64, 32], P('gy', 'gx'), may hold values from 0 to 1023, as said below
- occupancy: int32 [64, 4, 2], P('gx', 'gy'), may hold values from 0 to 1, as said below
- weight: bfloat16 [27, 96, 96], replicated, may hold values from -0.125 to 0.125
- w_in: bfloat16 [128, 96], replicated, may hold values from -0.5 to 0.5
- cotangent: bfloat16 [512, 32, 16, 96], P('gx', 'gy'), may hold values from -6 to 6
Outputs:
- point_feat: bfloat16 [4, 64, 64, 32, 96], P('gy', 'gx')
- point_grad: bfloat16 [4, 64, 64, 32, 128], P('gy', 'gx')
- weight_grad: float32 [27, 96, 96], replicated
Inputs may be any that keep to these rules, and one draw needn't show every extreme that they name: `counts`: in each gy row one owner receives 32 rows from every source. `voxels`: every slot's voxel lies in an occupied block of its owner tile. `occupancy`: every tile has at least one occupied block.
All inputs are finite; a program needn't handle non-finite values.
Results may differ from a plain program's by a relative error of at most 0.01.
Values may be sent and summed in bfloat16 or wider, within the bound.
A program may use at most 64 MiB of HBM per device.

v0:
```python
import jax
import jax.numpy as jnp
from jax import lax
from jax.sharding import PartitionSpec as P


def padded_2(block, sides, width):
    for axis, dim in sides:
        count = lax.axis_size(axis)
        forward = [(i, i + 1) for i in range(count - 1)]
        backward = [(target, source) for source, target in forward]
        low = lax.ppermute(
            lax.slice_in_dim(block, block.shape[dim] - width, None, axis=dim), axis, forward
        )
        high = lax.ppermute(lax.slice_in_dim(block, 0, width, axis=dim), axis, backward)
        block = jnp.concatenate([low, block, high], axis=dim)
    return block


def pad_depth(field):
    return jnp.pad(field, ((0, 0), (0, 0), (1, 1), (0, 0)))


def forward_taps(padded, weight, depth, width):
    total = jnp.zeros((64 * depth, width), jnp.float32)
    for tap in range(27):
        a, b, c = (tap // 9, tap // 3 % 3, tap % 3)
        window = padded[a : a + 8, b : b + 8, c : c + depth].reshape(-1, width)
        total = total + jnp.dot(window, weight[tap], preferred_element_type=jnp.float32)
    return total


def weight_terms(padded, grad_flat, depth, width):
    terms = []
    for tap in range(27):
        a, b, c = (tap // 9, tap // 3 % 3, tap % 3)
        window = padded[a : a + 8, b : b + 8, c : c + depth].reshape(-1, width)
        terms.append(
            lax.dot_general(
                window, grad_flat, (((0,), (0,)), ((), ())), preferred_element_type=jnp.float32
            )
        )
    return jnp.stack(terms)


def backward_taps(padded, weight, depth, width):
    total = jnp.zeros((64 * depth, width), jnp.float32)
    for tap in range(27):
        a, b, c = (tap // 9, tap // 3 % 3, tap % 3)
        window = padded[2 - a : 10 - a, 2 - b : 10 - b, 2 - c : 2 - c + depth].reshape(-1, width)
        total = total + jnp.dot(window, weight[tap].T, preferred_element_type=jnp.float32)
    return total


def on_device(points, counts, voxels, occupancy, weight, w_in, cotangent):
    width = weight.shape[2]
    feat_width = points.shape[4]
    depth = cotangent.shape[2]
    shape_slots = voxels.shape
    slots = lax.broadcasted_iota(jnp.int32, shape_slots, 3)
    got_points, got_voxels, got_counts = (
        lax.all_to_all(points, "gx", split_axis=2, concat_axis=2, tiled=True),
        lax.all_to_all(voxels, "gx", split_axis=2, concat_axis=2, tiled=True),
        lax.all_to_all(counts, "gx", split_axis=2, concat_axis=2, tiled=True),
    )
    got_valid = (slots < got_counts[..., None]).astype(jnp.float32).reshape(-1, 1)
    proj = (
        jnp.dot(got_points.reshape(-1, feat_width), w_in, preferred_element_type=jnp.float32)
        * got_valid
    ).astype(jnp.bfloat16)
    flat_index = got_voxels.reshape(-1)
    column_mask = jnp.repeat(occupancy[0, 0], 8).astype(jnp.float32)
    mask = jnp.broadcast_to(column_mask[None, None, :, None], (8, 8, depth, 1))
    summed = (
        jnp.zeros((64 * depth, width), jnp.float32).at[flat_index].add(proj.astype(jnp.float32))
    )
    feature = (summed.reshape(8, 8, depth, width) * mask).astype(jnp.bfloat16)
    grad_masked = (cotangent.astype(jnp.float32) * mask).astype(jnp.bfloat16)
    feature_pad = pad_depth(padded_2(feature, (("gx", 0), ("gy", 1)), 1))
    grad_pad = pad_depth(padded_2(grad_masked, (("gx", 0), ("gy", 1)), 1))
    mask_flat = mask.reshape(-1, 1)
    output = (forward_taps(feature_pad, weight, depth, width) * mask_flat).astype(jnp.bfloat16)
    local_grad = weight_terms(feature_pad, grad_masked.reshape(-1, width), depth, width)
    weight_grad = lax.psum(local_grad, ("gx", "gy"))
    feature_grad = (backward_taps(grad_pad, weight, depth, width) * mask_flat).astype(jnp.bfloat16)
    out_rows = (output[flat_index].astype(jnp.float32) * got_valid).astype(jnp.bfloat16)
    grad_rows = feature_grad[flat_index]
    point_rows = jnp.dot(grad_rows, w_in.T, preferred_element_type=jnp.float32) * got_valid
    sent_point = point_rows.astype(jnp.bfloat16).reshape(shape_slots + (feat_width,))
    point_feat, point_grad = (
        lax.all_to_all(
            out_rows.reshape(shape_slots + (width,)), "gx", split_axis=2, concat_axis=2, tiled=True
        ),
        lax.all_to_all(sent_point, "gx", split_axis=2, concat_axis=2, tiled=True),
    )
    return (point_feat, point_grad, weight_grad)


def solution(mesh):
    placed = (
        P("gy", "gx", None, None, None),
        P("gy", "gx", None),
        P("gy", "gx", None, None),
        P("gx", "gy", None),
        P(),
        P(),
        P("gx", "gy", None, None),
    )
    return jax.shard_map(
        on_device,
        mesh=mesh,
        in_specs=placed,
        out_specs=(P("gy", "gx", None, None, None), P("gy", "gx", None, None, None), P()),
        check_vma=False,
    )
```

profile of v0, /device:TPU:1, one launch (start us, length us, event | category | flops | bytes accessed | tf_op | source)
XLA Modules:
  0.0 468.1 jit_solution(846735209724311216)
XLA Ops:
  7.2 1.4 copy.31
  8.5 15.1 %all-to-all-start.2 = ((s32[1,1,64]{1,0,2:T(1,128)}), s32[1,1,64]{1,0,2:T(1,128)S(1)}, u32[]{:S(2)}, u32[]{:S(2)}) async-start(s32[1,1,64]{1,0,2:T(1,128)} %copy.31), calls=%async_computation.2 | async-start | bytes 65536 | tf_op jit(solution)/shard_map/all_to_all | solution.py:64
  23.7 1.4 copy.29
  25.1 9.3 %all-to-all-done.2 = s32[1,1,64]{1,0,2:T(1,128)S(1)} async-done(((s32[1,1,64]{1,0,2:T(1,128)}), s32[1,1,64]{1,0,2:T(1,128)S(1)}, u32[]{:S(2)}, u32[]{:S(2)}) %all-to-all-start.2) | async-done | bytes 288 | tf_op jit(solution)/shard_map/all_to_all | solution.py:64
  34.4 4.6 all-to-all-start
  40.0 1.2 reduce.1
  41.4 8.4 %all-to-all-done = s32[1,1,64,32]{3,1,0,2:T(1,128)S(1)} async-done(((s32[1,1,64,32]{3,1,0,2:T(1,128)}), s32[1,1,64,32]{3,1,0,2:T(1,128)S(1)}, u32[]{:S(2)}, u32[]{:S(2)}) %all-to-all-start) | async-done | bytes 8224 | tf_op jit(solution)/shard_map/all_to_all | solution.py:63
  49.8 4.6 all-to-all-start.1
  55.9 13.2 %all-to-all-done.1 = bf16[1,1,64,32,128]{4,3,1,0,2:T(8,128)(2,1)S(1)} async-done(((bf16[1,1,64,32,128]{4,3,1,0,2:T(8,128)(2,1)}), bf16[1,1,64,32,128]{4,3,1,0,2:T(8,128)(2,1)S(1)}, u32[]{:S(2)}, u32[]{:S(2)}) %all-to-all-start.1) | async-done | bytes 524320 | tf_op jit(solution)/shard_map/all_to_all | solution.py:62
  69.8 11.6 %scatter_custom_fusion = f32[1024,96]{1,0:T(8,128)S(1)} fusion(s32[2048]{0:T(1024)S(1)} %bitcast.568, f32[2048,96]{1,0:T(8,128)S(1)} %copy.32, f32[]{:T(128)} %constant.1.clone.1), kind=kCustom, calls=%fused_computation.151 | custom fusion | flops 196608 | bytes 393220 | tf_op jit(solution)/shard_map/scatter-add | solution.py:75
  81.6 1.3 collective-permute-start.1
  82.9 5.5 %collective-permute-start = (bf16[1,8,16,96]{3,2,1,0:T(8,128)(2,1)S(1)}, bf16[1,8,16,96]{3,2,1,0:T(8,128)(2,1)S(1)}, u32[]{:S(2)}, u32[]{:S(2)}) collective-permute-start(bf16[1,8,16,96]{3,2,1,0:T(8,128)(2,1)S(1)} %get-tuple-element.71), channel_id=1, source_target_pairs={{0,4},{4,8},{8,12},{12,16},{16,20},{20,24},{24,28},{28,32},{32,36}... | collective-permute-start | bytes 73736 | tf_op jit(solution)/shard_map/ppermute | solution.py:12
  88.6 1.3 collective-permute-start.5
  89.9 5.5 %collective-permute-start.4 = (bf16[1,8,16,96]{3,2,1,0:T(8,128)(2,1)S(1)}, bf16[1,8,16,96]{3,2,1,0:T(8,128)(2,1)S(1)}, u32[]{:S(2)}, u32[]{:S(2)}) collective-permute-start(bf16[1,8,16,96]{3,2,1,0:T(8,128)(2,1)S(1)} %get-tuple-element.67), channel_id=1, source_target_pairs={{0,4},{4,8},{8,12},{12,16},{16,20},{20,24},{24,28},{28,32},{32,36}... | collective-permute-start | bytes 73736 | tf_op jit(solution)/shard_map/ppermute | solution.py:12
  95.4 8.8 %collective-permute-start.3 = (bf16[10,1,16,96]{3,2,1,0:T(8,128)(2,1)S(1)}, bf16[10,1,16,96]{3,2,1,0:T(8,128)(2,1)S(1)}, u32[]{:S(2)}, u32[]{:S(2)}) collective-permute-start(bf16[10,1,16,96]{3,2,1,0:T(8,128)(2,1)S(1)} %get-tuple-element.64), channel_id=1, source_target_pairs={{1,0},{2,1},{3,2},{5,4},{6,5},{7,6},{9,8},{10,9},{11,10},{13,12},{... | collective-permute-start | bytes 92168 | tf_op jit(solution)/shard_map/ppermute | solution.py:15
  104.2 2.1 collective-permute-start.2
  107.0 2.2 collective-permute-start.7
  109.2 3.5 collective-permute-start.6
  113.3 1.1 fusion.190
  122.1 6.2 %gather_fusion = bf16[2048,96]{1,0:T(8,128)(2,1)S(1)} fusion(bf16[1024,96]{1,0:T(8,128)(2,1)S(1)} %copy.34, s32[2048]{0:T(1024)S(1)} %broadcast_clamp_fusion), kind=kCustom, calls=%fused_computation | custom fusion | bytes 794624 | tf_op jit(solution)/shard_map/gather | solution.py:86
  128.3 1.1 fusion.39
  130.3 14.4 %all-to-all-start.3 = ((bf16[1,1,64,32,96]{4,3,1,0,2:T(8,128)(2,1)}), bf16[1,1,64,32,96]{4,3,1,0,2:T(8,128)(2,1)S(1)}, u32[]{:S(2)}, u32[]{:S(2)}) async-start(bf16[1,1,64,32,96]{4,3,1,0,2:T(8,128)(2,1)} %fusion.39), calls=%async_computation.3 | async-start | bytes 1048576 | tf_op jit(solution)/shard_map/all_to_all | solution.py:91
  145.0 1.1 fusion.189
  146.8 0.9 fusion.19
  154.7 0.9 fusion.16
  171.3 6.2 %gather_fusion.1 = bf16[2048,96]{1,0:T(8,128)(2,1)S(1)} fusion(bf16[1024,96]{1,0:T(8,128)(2,1)S(1)} %copy.36, s32[2048]{0:T(1024)S(1)} %broadcast_clamp_fusion), kind=kCustom, calls=%fused_computation.1 | custom fusion | bytes 794624 | tf_op jit(solution)/shard_map/gather | solution.py:87
  177.5 0.9 fusion.13
  179.3 1.2 fusion
  180.4 11.9 %all-to-all-start.4 = ((bf16[1,1,64,32,128]{4,3,1,0,2:T(8,128)(2,1)}), bf16[1,1,64,32,128]{4,3,1,0,2:T(8,128)(2,1)S(1)}, u32[]{:S(2)}, u32[]{:S(2)}) async-start(bf16[1,1,64,32,128]{4,3,1,0,2:T(8,128)(2,1)} %bitcast.89), calls=%async_computation.4 | async-start | bytes 1048576 | tf_op jit(solution)/shard_map/all_to_all | solution.py:94
  195.1 16.9 %all-to-all-done.4 = bf16[1,1,64,32,128]{4,3,1,0,2:T(8,128)(2,1)S(1)} async-done(((bf16[1,1,64,32,128]{4,3,1,0,2:T(8,128)(2,1)}), bf16[1,1,64,32,128]{4,3,1,0,2:T(8,128)(2,1)S(1)}, u32[]{:S(2)}, u32[]{:S(2)}) %all-to-all-start.4) | async-done | bytes 524320 | tf_op jit(solution)/shard_map/all_to_all | solution.py:94
  211.9 246.7 %all-reduce.4.cloned.1.call-done = f32[27,96,96]{2,1,0:T(8,128)} async-done(((f32[27,96,96]{2,1,0:T(8,128)}), f32[27,96,96]{2,1,0:T(8,128)}) %all-reduce.4.cloned.1.call-update) | async-done | bytes 995344 | tf_op jit(solution)/shard_map/psum | solution.py:84
  460.2 1.1 copy.98
  (133 shorter events, 42.0 us)
Async XLA Ops:
  7.2 61.9 %copy-start = (bf16[128,96]{0,1:T(8,128)(2,1)S(1)}, bf16[128,96]{0,1:T(8,128)(2,1)}, u32[]{:S(2)}) copy-start(bf16[128,96]{0,1:T(8,128)(2,1)} %param.12) | copy-start | bytes 73732
  8.5 25.9 %all-to-all-start.2 = ((s32[1,1,64]{1,0,2:T(1,128)}), s32[1,1,64]{1,0,2:T(1,128)S(1)}, u32[]{:S(2)}, u32[]{:S(2)}) async-start(s32[1,1,64]{1,0,2:T(1,128)} %copy.31), calls=%async_computation.2 | async-start | bytes 65536 | tf_op jit(solution)/shard_map/all_to_all | solution.py:64
  34.4 15.4 %all-to-all-start = ((s32[1,1,64,32]{3,1,0,2:T(1,128)}), s32[1,1,64,32]{3,1,0,2:T(1,128)S(1)}, u32[]{:S(2)}, u32[]{:S(2)}) async-start(s32[1,1,64,32]{3,1,0,2:T(1,128)} %copy.29), calls=%async_computation | async-start | bytes 65536 | tf_op jit(solution)/shard_map/all_to_all | solution.py:63
  49.8 19.3 %all-to-all-start.1 = ((bf16[1,1,64,32,128]{4,3,1,0,2:T(8,128)(2,1)}), bf16[1,1,64,32,128]{4,3,1,0,2:T(8,128)(2,1)S(1)}, u32[]{:S(2)}, u32[]{:S(2)}) async-start(bf16[1,1,64,32,128]{4,3,1,0,2:T(8,128)(2,1)} %bitcast.566), calls=%async_computation.1 | async-start | bytes 1048576 | tf_op jit(solution)/shard_map/all_to_all | solution.py:62
  69.4 12.0 %copy-start.3 = (bf16[8,8,16,96]{3,2,1,0:T(8,128)(2,1)S(1)}, bf16[8,8,16,96]{3,2,1,0:T(8,128)(2,1)}, u32[]{:S(2)}) copy-start(bf16[8,8,16,96]{3,2,1,0:T(8,128)(2,1)} %param.13) | copy-start | bytes 589828
  81.6 13.8 %collective-permute-start.1 = (bf16[1,8,16,96]{3,2,1,0:T(8,128)(2,1)S(1)}, bf16[1,8,16,96]{3,2,1,0:T(8,128)(2,1)S(1)}, u32[]{:S(2)}, u32[]{:S(2)}) collective-permute-start(bf16[1,8,16,96]{3,2,1,0:T(8,128)(2,1)S(1)} %get-tuple-element.72), channel_id=1, source_target_pairs={{4,0},{8,4},{12,8},{16,12},{20,16},{24,20},{28,24},{32,28},{36,32}... | collective-permute-start | bytes 73736 | tf_op jit(solution)/shard_map/ppermute | solution.py:15
  82.9 12.5 %collective-permute-start = (bf16[1,8,16,96]{3,2,1,0:T(8,128)(2,1)S(1)}, bf16[1,8,16,96]{3,2,1,0:T(8,128)(2,1)S(1)}, u32[]{:S(2)}, u32[]{:S(2)}) collective-permute-start(bf16[1,8,16,96]{3,2,1,0:T(8,128)(2,1)S(1)} %get-tuple-element.71), channel_id=1, source_target_pairs={{0,4},{4,8},{8,12},{12,16},{16,20},{20,24},{24,28},{28,32},{32,36}... | collective-permute-start | bytes 73736 | tf_op jit(solution)/shard_map/ppermute | solution.py:12
  88.6 17.8 %collective-permute-start.5 = (bf16[1,8,16,96]{3,2,1,0:T(8,128)(2,1)S(1)}, bf16[1,8,16,96]{3,2,1,0:T(8,128)(2,1)S(1)}, u32[]{:S(2)}, u32[]{:S(2)}) collective-permute-start(bf16[1,8,16,96]{3,2,1,0:T(8,128)(2,1)S(1)} %get-tuple-element.68), channel_id=1, source_target_pairs={{4,0},{8,4},{12,8},{16,12},{20,16},{24,20},{28,24},{32,28},{36,32}... | collective-permute-start | bytes 73736 | tf_op jit(solution)/shard_map/ppermute | solution.py:15
  89.9 16.5 %collective-permute-start.4 = (bf16[1,8,16,96]{3,2,1,0:T(8,128)(2,1)S(1)}, bf16[1,8,16,96]{3,2,1,0:T(8,128)(2,1)S(1)}, u32[]{:S(2)}, u32[]{:S(2)}) collective-permute-start(bf16[1,8,16,96]{3,2,1,0:T(8,128)(2,1)S(1)} %get-tuple-element.67), channel_id=1, source_target_pairs={{0,4},{4,8},{8,12},{12,16},{16,20},{20,24},{24,28},{28,32},{32,36}... | collective-permute-start | bytes 73736 | tf_op jit(solution)/shard_map/ppermute | solution.py:12
  95.4 17.5 %collective-permute-start.3 = (bf16[10,1,16,96]{3,2,1,0:T(8,128)(2,1)S(1)}, bf16[10,1,16,96]{3,2,1,0:T(8,128)(2,1)S(1)}, u32[]{:S(2)}, u32[]{:S(2)}) collective-permute-start(bf16[10,1,16,96]{3,2,1,0:T(8,128)(2,1)S(1)} %get-tuple-element.64), channel_id=1, source_target_pairs={{1,0},{2,1},{3,2},{5,4},{6,5},{7,6},{9,8},{10,9},{11,10},{13,12},{... | collective-permute-start | bytes 92168 | tf_op jit(solution)/shard_map/ppermute | solution.py:15
  104.2 8.7 %collective-permute-start.2 = (bf16[10,1,16,96]{3,2,1,0:T(8,128)(2,1)S(1)}, bf16[10,1,16,96]{3,2,1,0:T(8,128)(2,1)S(1)}, u32[]{:S(2)}, u32[]{:S(2)}) collective-permute-start(bf16[10,1,16,96]{3,2,1,0:T(8,128)(2,1)S(1)} %get-tuple-element.63), channel_id=1, source_target_pairs={{0,1},{1,2},{2,3},{4,5},{5,6},{6,7},{8,9},{9,10},{10,11},{12,13},{... | collective-permute-start | bytes 92168 | tf_op jit(solution)/shard_map/ppermute | solution.py:12
  107.0 37.7 %collective-permute-start.7 = (bf16[10,1,16,96]{3,2,1,0:T(8,128)(2,1)}, bf16[10,1,16,96]{3,2,1,0:T(8,128)(2,1)S(1)}, u32[]{:S(2)}, u32[]{:S(2)}) collective-permute-start(bf16[10,1,16,96]{3,2,1,0:T(8,128)(2,1)} %get-tuple-element.60), channel_id=1, source_target_pairs={{1,0},{2,1},{3,2},{5,4},{6,5},{7,6},{9,8},{10,9},{11,10},{13,12},{... | collective-permute-start | bytes 92168 | tf_op jit(solution)/shard_map/ppermute | solution.py:15
  109.2 35.5 %collective-permute-start.6 = (bf16[10,1,16,96]{3,2,1,0:T(8,128)(2,1)S(1)}, bf16[10,1,16,96]{3,2,1,0:T(8,128)(2,1)S(1)}, u32[]{:S(2)}, u32[]{:S(2)}) collective-permute-start(bf16[10,1,16,96]{3,2,1,0:T(8,128)(2,1)S(1)} %get-tuple-element.59), channel_id=1, source_target_pairs={{0,1},{1,2},{2,3},{4,5},{5,6},{6,7},{8,9},{9,10},{10,11},{12,13},{... | collective-permute-start | bytes 92168 | tf_op jit(solution)/shard_map/ppermute | solution.py:12
  113.3 1.1 copy-start.1
  130.3 50.1 %all-to-all-start.3 = ((bf16[1,1,64,32,96]{4,3,1,0,2:T(8,128)(2,1)}), bf16[1,1,64,32,96]{4,3,1,0,2:T(8,128)(2,1)S(1)}, u32[]{:S(2)}, u32[]{:S(2)}) async-start(bf16[1,1,64,32,96]{4,3,1,0,2:T(8,128)(2,1)} %fusion.39), calls=%async_computation.3 | async-start | bytes 1048576 | tf_op jit(solution)/shard_map/all_to_all | solution.py:91
  180.4 31.5 %all-to-all-start.4 = ((bf16[1,1,64,32,128]{4,3,1,0,2:T(8,128)(2,1)}), bf16[1,1,64,32,128]{4,3,1,0,2:T(8,128)(2,1)S(1)}, u32[]{:S(2)}, u32[]{:S(2)}) async-start(bf16[1,1,64,32,128]{4,3,1,0,2:T(8,128)(2,1)} %bitcast.89), calls=%async_computation.4 | async-start | bytes 1048576 | tf_op jit(solution)/shard_map/all_to_all | solution.py:94
  192.4 266.3 %all-reduce.4.cloned.1.call-start = ((), (), s32[]{:S(2)}) async-start(), calls=%async_computation.5 | async-start | bytes 2654208 | tf_op jit(solution)/shard_map/psum | solution.py:84
  458.6 1.6 copy-start.2
Sparse Core Ops, SparseCore 0:
  199.2 259.4 all-reduce.3
where the time goes:
time: 469 us; the launch traced here: 468 us
  waiting for transfers between devices  295 us (63%)
  starting transfers between devices  80.9 us (17%)
  matrix products  38.1 us (8%)
  local copies, waits for them, and re-layouts  22.7 us (5%)
  other arithmetic  17.2 us (4%)
  between operations  14.6 us (3%)
    psum x1, waiting for transfers between devices, on_device(): weight_grad = lax.psum(local_grad, ('gx', 'gy'))  247 us
    dot_general x27, matrix products, weight_terms(): lax.dot_general(window, grad_flat, (((0,), (0,)), ((), ())), preferred_el...  23.6 us
    all_to_all x1, waiting for transfers between devices, on_device(): lax.all_to_all(sent_point, 'gx', split_axis=2, concat_axis=2, tiled=True)  16.9 us
    ppermute x4, starting transfers between devices, padded_2(): lax.ppermute(lax.slice_in_dim(block, block.shape[dim] - width, None, axis...  16.6 us
    all_to_all x1, starting transfers between devices, on_device(): lax.all_to_all(counts, 'gx', split_axis=2, concat_axis=2, tiled=True)  15.1 us
    all_to_all x1, starting transfers between devices, on_device(): lax.all_to_all(out_rows.reshape(shape_slots + (width,)), 'gx', split_axis...  14.4 us
    ppermute x4, starting transfers between devices, padded_2(): lax.ppermute(lax.slice_in_dim(block, 0, width, axis=dim), axis, backward)  13.6 us
    all_to_all x1, waiting for transfers between devices, on_device(): lax.all_to_all(points, 'gx', split_axis=2, concat_axis=2, tiled=True)  13.2 us
  transfers between devices with their start and end apart: 14, of which 5 were waited for; matrix products, arithmetic and copies ran while one was open for 13% of the time, Pallas kernels for 0%

commit v1 on v0

--- a/solution.py
+++ b/solution.py
@@ -81,7 +81,8 @@
     mask_flat = mask.reshape(-1, 1)
     output = (forward_taps(feature_pad, weight, depth, width) * mask_flat).astype(jnp.bfloat16)
     local_grad = weight_terms(feature_pad, grad_masked.reshape(-1, width), depth, width)
-    weight_grad = lax.psum(local_grad, ("gx", "gy"))
+    all_rows = lax.psum(local_grad, "gy")
+    weight_grad = lax.psum(all_rows, "gx")
     feature_grad = (backward_taps(grad_pad, weight, depth, width) * mask_flat).astype(jnp.bfloat16)
     out_rows = (output[flat_index].astype(jnp.float32) * got_valid).astype(jnp.bfloat16)
     grad_rows = feature_grad[flat_index]

time: 469 us -> 923 us (1.97)
  the two profiles are of different devices: /device:TPU:1 before, /device:TPU:8 now
where the time goes in v1:
time: 923 us; the launch traced here: 922 us
  waiting for transfers between devices  747 us (81%)
  starting transfers between devices  76.2 us (8%)
  matrix products  38.8 us (4%)
  local copies, waits for them, and re-layouts  27.5 us (3%)
  other arithmetic  17.4 us (2%)
  between operations  14.7 us (2%)
    psum x1, waiting for transfers between devices, on_device(): weight_grad = lax.psum(all_rows, 'gx')  691 us
    dot_general x27, matrix products, weight_terms(): lax.dot_general(window, grad_flat, (((0,), (0,)), ((), ())), preferred_el...  23.6 us
    psum x1, waiting for transfers between devices, on_device(): all_rows = lax.psum(local_grad, 'gy')  22.4 us
  transfers between devices with their start and end apart: 15, of which 6 were waited for; matrix products, arithmetic and copies ran while one was open for 7% of the time, Pallas kernels for 0%

profile of v1, /device:TPU:8, one launch (start us, length us, event | category | flops | bytes accessed | tf_op | source)
XLA Modules:
  0.0 921.9 jit_solution(3263087479019215200)
XLA Ops:
  7.2 1.4 copy.31
  8.5 14.6 %all-to-all-start.2 = ((s32[1,1,64]{1,0,2:T(1,128)}), s32[1,1,64]{1,0,2:T(1,128)S(1)}, u32[]{:S(2)}, u32[]{:S(2)}) async-start(s32[1,1,64]{1,0,2:T(1,128)} %copy.31), calls=%async_computation.2 | async-start | bytes 65536 | tf_op jit(solution)/shard_map/all_to_all | solution.py:64
  23.1 1.4 copy.29
  24.5 9.5 %all-to-all-done.2 = s32[1,1,64]{1,0,2:T(1,128)S(1)} async-done(((s32[1,1,64]{1,0,2:T(1,128)}), s32[1,1,64]{1,0,2:T(1,128)S(1)}, u32[]{:S(2)}, u32[]{:S(2)}) %all-to-all-start.2) | async-done | bytes 288 | tf_op jit(solution)/shard_map/all_to_all | solution.py:64
  34.0 5.5 all-to-all-start
  40.5 1.2 reduce.1
  41.9 8.7 all-to-all-done
  50.6 5.5 all-to-all-start.1
  57.5 14.9 %all-to-all-done.1 = bf16[1,1,64,32,128]{4,3,1,0,2:T(8,128)(2,1)S(1)} async-done(((bf16[1,1,64,32,128]{4,3,1,0,2:T(8,128)(2,1)}), bf16[1,1,64,32,128]{4,3,1,0,2:T(8,128)(2,1)S(1)}, u32[]{:S(2)}, u32[]{:S(2)}) %all-to-all-start.1) | async-done | bytes 524320 | tf_op jit(solution)/shard_map/all_to_all | solution.py:62
  73.1 11.6 %scatter_custom_fusion = f32[1024,96]{1,0:T(8,128)S(1)} fusion(s32[2048]{0:T(1024)S(1)} %bitcast.568, f32[2048,96]{1,0:T(8,128)S(1)} %copy.32, f32[]{:T(128)} %constant.1.clone.1), kind=kCustom, calls=%fused_computation.151 | custom fusion | flops 196608 | bytes 393220 | tf_op jit(solution)/shard_map/scatter-add | solution.py:75
  84.9 3.6 collective-permute-start.1
  88.6 3.7 collective-permute-start
  92.5 4.5 collective-permute-start.5
  97.1 2.8 collective-permute-start.4
  99.9 1.3 collective-permute-start.3
  101.2 3.0 collective-permute-start.2
  104.3 1.0 collective-permute-done.4
  105.3 1.3 collective-permute-start.7
  106.6 3.2 collective-permute-start.6
  111.1 1.1 fusion.190
  119.9 6.2 gather_fusion
  126.1 1.1 fusion.39
  128.1 14.1 %all-to-all-start.3 = ((bf16[1,1,64,32,96]{4,3,1,0,2:T(8,128)(2,1)}), bf16[1,1,64,32,96]{4,3,1,0,2:T(8,128)(2,1)S(1)}, u32[]{:S(2)}, u32[]{:S(2)}) async-start(bf16[1,1,64,32,96]{4,3,1,0,2:T(8,128)(2,1)} %fusion.39), calls=%async_computation.3 | async-start | bytes 1048576 | tf_op jit(solution)/shard_map/all_to_all | solution.py:92
  142.8 2.0 fusion.189
  145.1 1.0 fusion.99
  146.2 0.9 fusion.19
  179.2 6.2 gather_fusion.1
  185.4 1.2 fusion
  186.5 12.7 %all-to-all-start.4 = ((bf16[1,1,64,32,128]{4,3,1,0,2:T(8,128)(2,1)}), bf16[1,1,64,32,128]{4,3,1,0,2:T(8,128)(2,1)S(1)}, u32[]{:S(2)}, u32[]{:S(2)}) async-start(bf16[1,1,64,32,128]{4,3,1,0,2:T(8,128)(2,1)} %bitcast.89), calls=%async_computation.4 | async-start | bytes 1048576 | tf_op jit(solution)/shard_map/all_to_all | solution.py:95
  199.3 22.4 %all-reduce.5.cloned.1.call-done = f32[27,96,96]{2,1,0:T(8,128)} async-done(((f32[27,96,96]{2,1,0:T(8,128)}), f32[27,96,96]{2,1,0:T(8,128)}) %all-reduce.5.cloned.1.call-update) | async-done | bytes 995344 | tf_op jit(solution)/shard_map/psum | solution.py:84
  221.7 690.7 %all-reduce.7.cloned.1.call-done = f32[27,96,96]{2,1,0:T(8,128)} async-done(((f32[27,96,96]{2,1,0:T(8,128)}), f32[27,96,96]{2,1,0:T(8,128)}) %all-reduce.7.cloned.1.call-update) | async-done | bytes 995344 | tf_op jit(solution)/shard_map/psum | solution.py:85
  914.0 1.1 copy.99
  (172 shorter events, 47.9 us)
Async XLA Ops:
  7.2 65.3 %copy-start = (bf16[128,96]{0,1:T(8,128)(2,1)S(1)}, bf16[128,96]{0,1:T(8,128)(2,1)}, u32[]{:S(2)}) copy-start(bf16[128,96]{0,1:T(8,128)(2,1)} %param.12) | copy-start | bytes 73732
  8.5 25.5 %all-to-all-start.2 = ((s32[1,1,64]{1,0,2:T(1,128)}), s32[1,1,64]{1,0,2:T(1,128)S(1)}, u32[]{:S(2)}, u32[]{:S(2)}) async-start(s32[1,1,64]{1,0,2:T(1,128)} %copy.31), calls=%async_computation.2 | async-start | bytes 65536 | tf_op jit(solution)/shard_map/all_to_all | solution.py:64
  34.0 16.5 %all-to-all-start = ((s32[1,1,64,32]{3,1,0,2:T(1,128)}), s32[1,1,64,32]{3,1,0,2:T(1,128)S(1)}, u32[]{:S(2)}, u32[]{:S(2)}) async-start(s32[1,1,64,32]{3,1,0,2:T(1,128)} %copy.29), calls=%async_computation | async-start | bytes 65536 | tf_op jit(solution)/shard_map/all_to_all | solution.py:63
  50.6 21.9 %all-to-all-start.1 = ((bf16[1,1,64,32,128]{4,3,1,0,2:T(8,128)(2,1)}), bf16[1,1,64,32,128]{4,3,1,0,2:T(8,128)(2,1)S(1)}, u32[]{:S(2)}, u32[]{:S(2)}) async-start(bf16[1,1,64,32,128]{4,3,1,0,2:T(8,128)(2,1)} %bitcast.566), calls=%async_computation.1 | async-start | bytes 1048576 | tf_op jit(solution)/shard_map/all_to_all | solution.py:62
  72.8 12.0 %copy-start.21 = (bf16[8,8,16,96]{3,2,1,0:T(8,128)(2,1)S(1)}, bf16[8,8,16,96]{3,2,1,0:T(8,128)(2,1)}, u32[]{:S(2)}) copy-start(bf16[8,8,16,96]{3,2,1,0:T(8,128)(2,1)} %param.13) | copy-start | bytes 589828
  84.9 14.9 %collective-permute-start.1 = (bf16[1,8,16,96]{3,2,1,0:T(8,128)(2,1)S(1)}, bf16[1,8,16,96]{3,2,1,0:T(8,128)(2,1)S(1)}, u32[]{:S(2)}, u32[]{:S(2)}) collective-permute-start(bf16[1,8,16,96]{3,2,1,0:T(8,128)(2,1)S(1)} %get-tuple-element.72), channel_id=1, source_target_pairs={{4,0},{8,4},{12,8},{16,12},{20,16},{24,20},{28,24},{32,28},{36,32}... | collective-permute-start | bytes 73736 | tf_op jit(solution)/shard_map/ppermute | solution.py:15
  88.6 11.3 %collective-permute-start = (bf16[1,8,16,96]{3,2,1,0:T(8,128)(2,1)S(1)}, bf16[1,8,16,96]{3,2,1,0:T(8,128)(2,1)S(1)}, u32[]{:S(2)}, u32[]{:S(2)}) collective-permute-start(bf16[1,8,16,96]{3,2,1,0:T(8,128)(2,1)S(1)} %get-tuple-element.71), channel_id=1, source_target_pairs={{0,4},{4,8},{8,12},{12,16},{16,20},{20,24},{24,28},{28,32},{32,36}... | collective-permute-start | bytes 73736 | tf_op jit(solution)/shard_map/ppermute | solution.py:12
  92.5 11.8 %collective-permute-start.5 = (bf16[1,8,16,96]{3,2,1,0:T(8,128)(2,1)S(1)}, bf16[1,8,16,96]{3,2,1,0:T(8,128)(2,1)S(1)}, u32[]{:S(2)}, u32[]{:S(2)}) collective-permute-start(bf16[1,8,16,96]{3,2,1,0:T(8,128)(2,1)S(1)} %get-tuple-element.68), channel_id=1, source_target_pairs={{4,0},{8,4},{12,8},{16,12},{20,16},{24,20},{28,24},{32,28},{36,32}... | collective-permute-start | bytes 73736 | tf_op jit(solution)/shard_map/ppermute | solution.py:15
  97.1 8.2 collective-permute-start.4
  99.9 10.8 %collective-permute-start.3 = (bf16[10,1,16,96]{3,2,1,0:T(8,128)(2,1)S(1)}, bf16[10,1,16,96]{3,2,1,0:T(8,128)(2,1)S(1)}, u32[]{:S(2)}, u32[]{:S(2)}) collective-permute-start(bf16[10,1,16,96]{3,2,1,0:T(8,128)(2,1)S(1)} %get-tuple-element.64), channel_id=1, source_target_pairs={{1,0},{2,1},{3,2},{5,4},{6,5},{7,6},{9,8},{10,9},{11,10},{13,12},{... | collective-permute-start | bytes 92168 | tf_op jit(solution)/shard_map/ppermute | solution.py:15
  101.2 9.5 %collective-permute-start.2 = (bf16[10,1,16,96]{3,2,1,0:T(8,128)(2,1)S(1)}, bf16[10,1,16,96]{3,2,1,0:T(8,128)(2,1)S(1)}, u32[]{:S(2)}, u32[]{:S(2)}) collective-permute-start(bf16[10,1,16,96]{3,2,1,0:T(8,128)(2,1)S(1)} %get-tuple-element.63), channel_id=1, source_target_pairs={{0,1},{1,2},{2,3},{4,5},{5,6},{6,7},{8,9},{9,10},{10,11},{12,13},{... | collective-permute-start | bytes 92168 | tf_op jit(solution)/shard_map/ppermute | solution.py:12
  105.3 37.2 %collective-permute-start.7 = (bf16[10,1,16,96]{3,2,1,0:T(8,128)(2,1)S(1)}, bf16[10,1,16,96]{3,2,1,0:T(8,128)(2,1)S(1)}, u32[]{:S(2)}, u32[]{:S(2)}) collective-permute-start(bf16[10,1,16,96]{3,2,1,0:T(8,128)(2,1)S(1)} %get-tuple-element.60), channel_id=1, source_target_pairs={{1,0},{2,1},{3,2},{5,4},{6,5},{7,6},{9,8},{10,9},{11,10},{13,12},{... | collective-permute-start | bytes 92168 | tf_op jit(solution)/shard_map/ppermute | solution.py:15
  106.6 35.9 %collective-permute-start.6 = (bf16[10,1,16,96]{3,2,1,0:T(8,128)(2,1)S(1)}, bf16[10,1,16,96]{3,2,1,0:T(8,128)(2,1)S(1)}, u32[]{:S(2)}, u32[]{:S(2)}) collective-permute-start(bf16[10,1,16,96]{3,2,1,0:T(8,128)(2,1)S(1)} %get-tuple-element.59), channel_id=1, source_target_pairs={{0,1},{1,2},{2,3},{4,5},{5,6},{6,7},{8,9},{9,10},{10,11},{12,13},{... | collective-permute-start | bytes 92168 | tf_op jit(solution)/shard_map/ppermute | solution.py:12
  111.1 1.1 copy-start.1
  128.1 58.4 %all-to-all-start.3 = ((bf16[1,1,64,32,96]{4,3,1,0,2:T(8,128)(2,1)}), bf16[1,1,64,32,96]{4,3,1,0,2:T(8,128)(2,1)S(1)}, u32[]{:S(2)}, u32[]{:S(2)}) async-start(bf16[1,1,64,32,96]{4,3,1,0,2:T(8,128)(2,1)} %fusion.39), calls=%async_computation.3 | async-start | bytes 1048576 | tf_op jit(solution)/shard_map/all_to_all | solution.py:92
  142.2 79.5 %all-reduce.5.cloned.1.call-start = ((), (), s32[]{:S(2)}) async-start(), calls=%async_computation.5 | async-start | bytes 2654208 | tf_op jit(solution)/shard_map/psum | solution.py:84
  169.7 1.0 copy-start.2
  169.7 1.1 copy-start.20
  170.3 1.0 copy-start.16
  171.6 1.0 copy-start.14
  172.7 1.0 copy-start.12
  173.4 1.0 copy-start.11
  173.9 1.0 copy-start.10
  174.6 1.0 copy-start.9
  175.1 1.0 copy-start.8
  175.8 1.0 copy-start.7
  176.3 1.0 copy-start.6
  176.6 1.0 copy-start.19
  177.0 1.0 copy-start.5
  186.5 35.2 %all-to-all-start.4 = ((bf16[1,1,64,32,128]{4,3,1,0,2:T(8,128)(2,1)}), bf16[1,1,64,32,128]{4,3,1,0,2:T(8,128)(2,1)S(1)}, u32[]{:S(2)}, u32[]{:S(2)}) async-start(bf16[1,1,64,32,128]{4,3,1,0,2:T(8,128)(2,1)} %bitcast.89), calls=%async_computation.4 | async-start | bytes 1048576 | tf_op jit(solution)/shard_map/all_to_all | solution.py:95
  199.2 713.2 %all-reduce.7.cloned.1.call-start = ((), (), s32[]{:S(2)}) async-start(), calls=%async_computation.6 | async-start | bytes 2654208 | tf_op jit(solution)/shard_map/psum | solution.py:85
  912.4 1.6 copy-start.3
  (5 other events, 4.8 us)
Sparse Core Ops, SparseCore 0:
  169.1 52.5 all-reduce.4
  224.3 688.0 all-reduce.6
